TPU v7x, 256 devices: a whole 4x4x8 slice. The times are simulated.
256 devices in a mesh: ep: 32 (over y, z_hi, core), dp: 8 (over z_lo, x).
Axes of the slice: x: 4, y: 4, z: 8 (z_hi: 4, z_lo: 2; z = z_hi * 2 + z_lo), core: 2. Of those that a mesh axis runs over, the one named last changes fastest.
Arguments:
- gradients: float32 [8, 4096, 7168], P('dp', 'ep'), may hold values from -18 to 18
- master_rows: float32 [32, 192, 7168], P('ep', 'dp'), may hold values from -0.24 to 0.24
- first_moment: float32 [32, 192, 7168], P('ep', 'dp'), may hold values from -2 to 2
- second_moment: float32 [32, 192, 7168], P('ep', 'dp'), may hold values from 0.1 to 1
- shard_rows: int32 [32, 8], replicated, may hold values from 1 to 24, as said below
- move_partner: int32 [32], replicated, may hold values from 0 to 31, as said below
Outputs:
- new_master: float32 [32, 192, 7168], P('ep', 'dp')
- new_first: float32 [32, 192, 7168], P('ep', 'dp')
- new_second: float32 [32, 192, 7168], P('ep', 'dp')
- placed_params: bfloat16 [4096, 7168], P('ep')
Inputs may be any that keep to these rules, and one draw needn't show every extreme that they name: `shard_rows`: in each row the shards own consecutive runs of the 128 flat rows in order, each at least one row, summing to 128; the largest of each row is exactly 24. move_partner[i] is i or i with one binary digit flipped; that digit is the same for every i that moves; move_partner[move_partner[i]] == i.
All inputs are finite; a program needn't handle non-finite values.
Results may differ from a plain program's by a relative error of at most 0.014.
Values may be sent and summed in bfloat16 or wider, within the bound.
No kernel may reach another device: no remote copies, remote signals or barrier semaphores. Data moves between devices by JAX's collectives and lax.ppermute only.
A program may use at most 128 MiB of HBM per device.

v0:
```python
import jax
import jax.numpy as jnp
from jax import lax
from jax.experimental import pallas as pl
from jax.experimental.pallas import tpu as pltpu
from jax.sharding import PartitionSpec as P

beta_one = 0.9
beta_two = 0.95
learn_rate = 0.02
weight_decay = 0.1
epsilon = 1e-08
correct_one = 1.0 - 0.9**10
correct_two = 1.0 - 0.95**10

orders = ((4, 1, 3), (1, 3, 4), (3, 4, 1))
vmem_bytes = 48 * 1024 * 1024


def flipped_by(array, axis, mask):
    return lax.ppermute(array, axis, [(i, i ^ mask) for i in range(lax.axis_size(axis))])


def adam_step(grad_rows, weights, first, second, live):
    first_new = beta_one * first + (1.0 - beta_one) * grad_rows
    second_new = beta_two * second + (1.0 - beta_two) * grad_rows * grad_rows
    ratio = first_new / correct_one / (jnp.sqrt(second_new / correct_two) + epsilon)
    updated = weights - learn_rate * (ratio + weight_decay * weights)
    return (
        jnp.where(live, updated, 0.0),
        jnp.where(live, first_new, 0.0),
        jnp.where(live, second_new, 0.0),
    )


def slots_to_rows(rows_ref, ep_index, dp_index, order, capacity, flat_count):
    shards = rows_ref.shape[0]
    counts = [rows_ref[k, ep_index] for k in range(shards)]
    starts = [jnp.int32(0)]
    for k in range(shards - 1):
        starts.append(starts[-1] + counts[k])
    slot = lax.broadcasted_iota(jnp.int32, (capacity, flat_count), 0)
    flat = lax.broadcasted_iota(jnp.int32, (capacity, flat_count), 1)
    blocks = []
    for p in range(shards):
        k = dp_index ^ ((p >> 2 & 1) * order[0] ^ (p >> 1 & 1) * order[1] ^ (p & 1) * order[2])
        start, count = starts[0], counts[0]
        for j in range(1, shards):
            start = jnp.where(k == j, starts[j], start)
            count = jnp.where(k == j, counts[j], count)
        blocks.append(jnp.where((flat - slot == start) & (slot < count), 1.0, 0.0))
    return jnp.concatenate(blocks, axis=0)


smem_spec = pl.BlockSpec(memory_space=pltpu.SMEM)
vmem_spec = pl.BlockSpec(memory_space=pltpu.VMEM)
params = pltpu.CompilerParams(vmem_limit_bytes=vmem_bytes)


def pack_kernel(cuts, capacity, place_ref, rows_ref, grad_ref, *refs):
    outs, (columns_ref, sems) = refs[:6], refs[6:]
    flat_count = grad_ref.shape[1]
    copies = []
    for g in range(3):
        part = pl.ds(cuts[g], cuts[g + 1] - cuts[g])
        copies.append(pltpu.make_async_copy(grad_ref.at[0, :, part], columns_ref.at[:, part], sems.at[g]))
        copies[-1].start()
    half = 4 * capacity
    for g in range(3):
        hot = slots_to_rows(rows_ref, place_ref[0], place_ref[1], orders[g], capacity, flat_count)
        hot = hot.astype(jnp.bfloat16)
        copies[g].wait()
        columns = columns_ref[:, cuts[g] : cuts[g + 1]].astype(jnp.bfloat16)
        packed = jnp.dot(hot, columns, preferred_element_type=jnp.float32).astype(jnp.bfloat16)
        outs[g][...] = packed[half:]
        outs[3 + g][...] = packed[:half]


def pack(where, rows_by_shard, gradients, cuts, capacity):
    flat_count, width = gradients.shape[1:]
    shapes = [
        jax.ShapeDtypeStruct((4 * capacity, cuts[g + 1] - cuts[g]), jnp.bfloat16) for g in (0, 1, 2, 0, 1, 2)
    ]
    return pl.pallas_call(
        lambda *refs: pack_kernel(cuts, capacity, *refs),
        in_specs=[smem_spec, smem_spec, pl.BlockSpec(memory_space=pltpu.HBM)],
        out_specs=[vmem_spec] * 6,
        out_shape=shapes,
        scratch_shapes=[pltpu.VMEM((flat_count, width), jnp.float32), pltpu.SemaphoreType.DMA((3,))],
        compiler_params=params,
        name="pack",
    )(where, rows_by_shard, gradients)


def sum_kernel(*refs):
    kept, arrived, outs = refs[:3], refs[3:6], refs[6:]
    rest = kept[0].shape[0] // 2
    for g in range(3):
        outs[g][...] = (
            kept[g][rest:].astype(jnp.float32) + arrived[g][rest:].astype(jnp.float32)
        ).astype(jnp.bfloat16)
        outs[3 + g][...] = kept[g][:rest].astype(jnp.float32) + arrived[g][:rest].astype(jnp.float32)


def summed(kept, arrived):
    shapes = [
        jax.ShapeDtypeStruct((k.shape[0] // 2, k.shape[1]), dtype)
        for dtype in (jnp.bfloat16, jnp.float32)
        for k in kept
    ]
    outs = pl.pallas_call(
        sum_kernel,
        in_specs=[vmem_spec] * 6,
        out_specs=[vmem_spec] * 6,
        out_shape=shapes,
        compiler_params=params,
        name="sums",
    )(*kept, *arrived)
    return outs[:3], outs[3:]


def place_kernel(cuts, capacity, place_ref, rows_ref, *refs):
    here, arrived, out_ref = refs[:3], refs[3:6], refs[6]
    half = 4 * capacity
    for g in range(3):
        hot = slots_to_rows(rows_ref, place_ref[2], place_ref[1], orders[g], capacity, out_ref.shape[0])
        hot = hot.T.astype(jnp.bfloat16)
        total = jnp.dot(hot[:, :half], here[g][...], preferred_element_type=jnp.float32)
        total += jnp.dot(hot[:, half:], arrived[g][...], preferred_element_type=jnp.float32)
        out_ref[:, cuts[g] : cuts[g + 1]] = total.astype(jnp.bfloat16)


def place(where, rows_by_shard, here, arrived, cuts, capacity, flat_count):
    return pl.pallas_call(
        lambda *refs: place_kernel(cuts, capacity, *refs),
        in_specs=[smem_spec, smem_spec] + [vmem_spec] * 6,
        out_shape=jax.ShapeDtypeStruct((flat_count, cuts[-1]), jnp.bfloat16),
        compiler_params=params,
        name="place",
    )(where, rows_by_shard, *here, *arrived)


def body(gradients, master_rows, first_moment, second_moment, shard_rows, move_partner):
    capacity = master_rows.shape[1]
    flat_count, width = gradients.shape[1:]
    lanes = width // 128
    cuts = [128 * (lanes * i // 3) for i in range(4)]
    dp_index = lax.axis_index("dp")
    ep_index = lax.axis_index("ep")
    ep_all = jnp.arange(move_partner.shape[0], dtype=jnp.int32)
    where = jnp.stack([ep_index, dp_index]).astype(jnp.int32)

    rows_by_shard = shard_rows.T
    packed = pack(where, rows_by_shard, gradients, cuts, capacity)
    sent, kept = packed[:3], packed[3:]
    for step in range(3):
        arrived = [flipped_by(sent[g], "dp", orders[g][step]) for g in range(3)]
        if step < 2:
            sent, kept = summed(kept, arrived)
    grad_own = jnp.concatenate([k + a.astype(jnp.float32) for k, a in zip(kept, arrived)], axis=1) / 8

    partner = jnp.sum(jnp.where(ep_all == ep_index, move_partner, 0))
    own_counts = jnp.sum(jnp.where((ep_all == ep_index)[:, None], shard_rows, 0), axis=0)
    own_count = jnp.sum(jnp.where(jnp.arange(8, dtype=jnp.int32) == dp_index, own_counts, 0))
    live = (jnp.arange(capacity, dtype=jnp.int32) < own_count)[:, None]
    moves = partner != ep_index
    flips = jnp.bitwise_xor(move_partner, ep_all)
    bits = move_partner.shape[0].bit_length() - 1
    which_bit = jnp.max(sum((flips >= 1 << b).astype(jnp.int32) for b in range(1, bits)))

    updated, first_new, second_new = adam_step(
        grad_own, master_rows[0], first_moment[0], second_moment[0], live
    )

    def relocated(apart, arrays):
        return [flipped_by(a, "ep", 1 << apart) for a in arrays]

    sent_master = updated.astype(jnp.bfloat16)
    (there,) = lax.switch(
        which_bit, [lambda o, b=b: relocated(b, o) for b in range(bits)], [sent_master]
    )
    narrow = jnp.where(moves, there, sent_master)
    here = [narrow[:, cuts[g] : cuts[g + 1]] for g in range(3)]
    for step in range(2):
        arrived = [flipped_by(here[g], "dp", orders[g][2 - step]) for g in range(3)]
        arrived = lax.optimization_barrier(arrived)
        here = [jnp.concatenate(pair, axis=0) for pair in zip(here, arrived)]

    def last(apart, operands):
        here, moments = operands
        arrived = [flipped_by(here[g], "dp", orders[g][0]) for g in range(3)]
        return arrived, relocated(apart, moments)

    moments = [first_new.astype(jnp.bfloat16), second_new.astype(jnp.bfloat16)]
    arrived, moments = lax.switch(
        which_bit, [lambda o, b=b: last(b, o) for b in range(bits)], (here, moments)
    )
    placed = place(
        jnp.stack([ep_index, dp_index, partner]).astype(jnp.int32),
        rows_by_shard,
        here,
        arrived,
        cuts,
        capacity,
        flat_count,
    )
    new_master, new_first, new_second = [
        jnp.where(moves, arrived.astype(jnp.float32), own)[None]
        for arrived, own in ((there, updated), (moments[0], first_new), (moments[1], second_new))
    ]
    return new_master, new_first, new_second, placed


def solution(mesh):
    placed = (
        P("dp", "ep", None),
        P("ep", "dp", None),
        P("ep", "dp", None),
        P("ep", "dp", None),
        P(),
        P(),
    )
    return jax.shard_map(
        body,
        mesh=mesh,
        in_specs=placed,
        out_specs=(P("ep", "dp", None), P("ep", "dp", None), P("ep", "dp", None), P("ep", None)),
        check_vma=False,
    )
```

profile of v0, /device:TPU:2, one launch (start us, length us, event | category | flops | bytes accessed | tf_op | source)
XLA Modules:
  0.0 92.7 jit_solution(4524879131566844262)
XLA Ops:
  1.4 3.1 %pack.1 = (bf16[96,2304]{1,0:T(8,128)(2,1)S(1)}, bf16[96,2432]{1,0:T(8,128)(2,1)S(1)}, bf16[96,2432]{1,0:T(8,128)(2,1)S(1)}, bf16[96,2304]{1,0:T(8,128)(2,1)S(1)...) custom-call(s32[2]{0:T(128)S(1)} %pad_add_fusion.refs_0_, s32[8,32]{1,0:T(8,128)S(1)} %bitcast.40, ...), custom_call_target="tpu_custom_call" | custom-call | tf_op jit(solution)/shard_map/pack/pallas_call | solution.py:84
  4.6 2.4 %collective-permute-start.31 = (bf16[96,2432]{1,0:T(8,128)(2,1)S(1)}, bf16[96,2432]{1,0:T(8,128)(2,1)S(1)}, u32[]{:S(2)}, u32[]{:S(2)}) collective-permute-start(bf16[96,2432]{1,0:T(8,128)(2,1)S(1)} %get-tuple-element.146), channel_id=1, source_target_pairs={{0,1},{1,0},{2,3},{3,2},{4,5},{5,4},{6,7},{7,6},{8,9},{9,8},{10,11... | collective-permute-start | bytes 1400840 | tf_op jit(solution)/shard_map/ppermute | solution.py:21
  7.3 1.9 %collective-permute-start.30 = (bf16[96,2304]{1,0:T(8,128)(2,1)S(1)}, bf16[96,2304]{1,0:T(8,128)(2,1)S(1)}, u32[]{:S(2)}, u32[]{:S(2)}) collective-permute-start(bf16[96,2304]{1,0:T(8,128)(2,1)S(1)} %get-tuple-element.145), channel_id=1, source_target_pairs={{0,4},{1,5},{2,6},{3,7},{4,0},{5,1},{6,2},{7,3},{8,12},{9,13},{10,... | collective-permute-start | bytes 1327112 | tf_op jit(solution)/shard_map/ppermute | solution.py:21
  10.0 8.9 %collective-permute-done.30.refs_3_ = bf16[96,2304]{1,0:T(8,128)(2,1)S(1)} collective-permute-done((bf16[96,2304]{1,0:T(8,128)(2,1)S(1)}, bf16[96,2304]{1,0:T(8,128)(2,1)S(1)}, u32[]{:S(2)}, u32[]{:S(2)}) %collective-permute-start.30) | collective-permute-done | bytes 442400 | tf_op jit(solution)/shard_map/ppermute | solution.py:21
  19.9 1.9 %collective-permute-start.35 = (bf16[48,2432]{1,0:T(8,128)(2,1)S(1)}, bf16[48,2432]{1,0:T(8,128)(2,1)S(1)}, u32[]{:S(2)}, u32[]{:S(2)}) collective-permute-start(bf16[48,2432]{1,0:T(8,128)(2,1)S(1)} %get-tuple-element.153), channel_id=1, source_target_pairs={{0,4},{1,5},{2,6},{3,7},{4,0},{5,1},{6,2},{7,3},{8,12},{9,13},{10,... | collective-permute-start | bytes 700424 | tf_op jit(solution)/shard_map/ppermute | solution.py:21
  23.2 2.7 %collective-permute-start.33 = (bf16[48,2304]{1,0:T(8,128)(2,1)S(1)}, bf16[48,2304]{1,0:T(8,128)(2,1)S(1)}, u32[]{:S(2)}, u32[]{:S(2)}) collective-permute-start(bf16[48,2304]{1,0:T(8,128)(2,1)S(1)} %get-tuple-element.151), channel_id=1, source_target_pairs={{0,1},{1,0},{2,3},{3,2},{4,5},{5,4},{6,7},{7,6},{8,9},{9,8},{10,11... | collective-permute-start | bytes 663560 | tf_op jit(solution)/shard_map/ppermute | solution.py:21
  26.7 3.2 %collective-permute-done.33.refs_3_ = bf16[48,2304]{1,0:T(8,128)(2,1)S(1)} collective-permute-done((bf16[48,2304]{1,0:T(8,128)(2,1)S(1)}, bf16[48,2304]{1,0:T(8,128)(2,1)S(1)}, u32[]{:S(2)}, u32[]{:S(2)}) %collective-permute-start.33) | collective-permute-done | bytes 221216 | tf_op jit(solution)/shard_map/ppermute | solution.py:21
  31.7 2.6 %collective-permute-start.38 = (bf16[24,2432]{1,0:T(8,128)(2,1)S(1)}, bf16[24,2432]{1,0:T(8,128)(2,1)S(1)}, u32[]{:S(2)}, u32[]{:S(2)}) collective-permute-start(bf16[24,2432]{1,0:T(8,128)(2,1)S(1)} %get-tuple-element.159), channel_id=1, source_target_pairs={{0,1},{1,0},{2,3},{3,2},{4,5},{5,4},{6,7},{7,6},{8,9},{9,8},{10,11... | collective-permute-start | bytes 350216 | tf_op jit(solution)/shard_map/ppermute | solution.py:21
  38.7 9.3 %conditional.8 = (bf16[24,7168]{1,0:T(8,128)(2,1)}, bf16[24,7168]{1,0:T(8,128)(2,1)}) conditional(s32[]{:T(128)} %clamp.4, bf16[24,7168]{1,0:T(8,128)(2,1)} %get-tuple-element.188, bf16[24,7168]{1,0:T(8,128)(2,1)} %get-tuple-element.188, bf16[24,7168]{1,0:T(8,128)(2,1)} %get-tuple-element.188, ...), branch_computations={%region_4.5_spmd, %region_5.6_spmd, %region_6.7_spmd, %region_7.8_... | conditional | bytes 2064440
  40.3 6.0 %collective-permute-done.3 = bf16[24,7168]{1,0:T(8,128)(2,1)} collective-permute-done((bf16[24,7168]{1,0:T(8,128)(2,1)}, bf16[24,7168]{1,0:T(8,128)(2,1)}, u32[]{:S(2)}, u32[]{:S(2)}) %collective-permute-start.3) | collective-permute-done | bytes 344096 | tf_op jit(solution)/shard_map/cond/branch_3_fun/ppermute | solution.py:21
  46.2 1.8 %copy.17 = bf16[24,7168]{1,0:T(8,128)(2,1)} copy(bf16[24,7168]{1,0:T(8,128)(2,1)} %collective-permute-done.3) | data formatting | bytes 688128
  49.2 2.1 %collective-permute-start.41 = (bf16[24,2432]{1,0:T(8,128)(2,1)S(1)}, bf16[24,2432]{1,0:T(8,128)(2,1)S(1)}, u32[]{:S(2)}, u32[]{:S(2)}) collective-permute-start(bf16[24,2432]{1,0:T(8,128)(2,1)S(1)} %get-tuple-element.194), channel_id=1, source_target_pairs={{0,1},{1,0},{2,3},{3,2},{4,5},{5,4},{6,7},{7,6},{8,9},{9,8},{10,11... | collective-permute-start | bytes 350216 | tf_op jit(solution)/shard_map/ppermute | solution.py:21
  51.3 1.7 %collective-permute-start.40 = (bf16[24,2432]{1,0:T(8,128)(2,1)S(1)}, bf16[24,2432]{1,0:T(8,128)(2,1)S(1)}, u32[]{:S(2)}, u32[]{:S(2)}) collective-permute-start(bf16[24,2432]{1,0:T(8,128)(2,1)S(1)} %get-tuple-element.195), channel_id=1, source_target_pairs={{0,4},{1,5},{2,6},{3,7},{4,0},{5,1},{6,2},{7,3},{8,12},{9,13},{10,... | collective-permute-start | bytes 350216 | tf_op jit(solution)/shard_map/ppermute | solution.py:21
  53.0 1.7 %collective-permute-start.39 = (bf16[24,2304]{1,0:T(8,128)(2,1)S(1)}, bf16[24,2304]{1,0:T(8,128)(2,1)S(1)}, u32[]{:S(2)}, u32[]{:S(2)}) collective-permute-start(bf16[24,2304]{1,0:T(8,128)(2,1)S(1)} %slice.12), channel_id=1, source_target_pairs={{0,3},{1,2},{2,1},{3,0},{4,7},{5,6},{6,5},{7,4},{8,11},{9,10},{10,... | collective-permute-start | bytes 331784 | tf_op jit(solution)/shard_map/ppermute | solution.py:21
  55.5 3.2 %collective-permute-done.39 = bf16[24,2304]{1,0:T(8,128)(2,1)S(1)} collective-permute-done((bf16[24,2304]{1,0:T(8,128)(2,1)S(1)}, bf16[24,2304]{1,0:T(8,128)(2,1)S(1)}, u32[]{:S(2)}, u32[]{:S(2)}) %collective-permute-start.39) | collective-permute-done | bytes 110624 | tf_op jit(solution)/shard_map/ppermute | solution.py:21
  62.3 1.9 %fusion.5 = f32[1,24,7168]{2,1,0:T(8,128)} fusion(f32[24,7168]{1,0:T(8,128)S(1)} %get-tuple-element.189, bf16[24,7168]{1,0:T(8,128)(2,1)} %get-tuple-element.178, pred[]{:T(512)S(6)} %ne.3), kind=kLoop, calls=%fused_computation.13 | loop fusion | flops 344064 | bytes 1720321 | tf_op jit(solution)/shard_map/broadcast_in_dim | solution.py:208
  64.2 2.9 %collective-permute-done.42 = bf16[48,2304]{1,0:T(8,128)(2,1)S(1)} collective-permute-done((bf16[48,2304]{1,0:T(8,128)(2,1)S(1)}, bf16[48,2304]{1,0:T(8,128)(2,1)S(1)}, u32[]{:S(2)}, u32[]{:S(2)}) %collective-permute-start.42) | collective-permute-done | bytes 221216 | tf_op jit(solution)/shard_map/ppermute | solution.py:21
  67.1 1.6 %collective-permute-done.44 = bf16[48,2432]{1,0:T(8,128)(2,1)S(1)} collective-permute-done((bf16[48,2432]{1,0:T(8,128)(2,1)S(1)}, bf16[48,2432]{1,0:T(8,128)(2,1)S(1)}, u32[]{:S(2)}, u32[]{:S(2)}) %collective-permute-start.44) | collective-permute-done | bytes 233504 | tf_op jit(solution)/shard_map/ppermute | solution.py:21
  70.6 15.6 %conditional.9 = (bf16[96,2304]{1,0:T(8,128)(2,1)}, bf16[96,2432]{1,0:T(8,128)(2,1)}, bf16[96,2432]{1,0:T(8,128)(2,1)}, bf16[24,7168]{1,0:T(8,128)(2,1)}, bf16[24,7168]{1,0:T(8,128)(2,1)}) conditional(s32[]{:T(128)} %clamp.4, (bf16[96,2304]{1,0:T(8,128)(2,1)S(1)}, bf16[96,2432]{1,0:T(8,128)(2,1)S(1)}, ...), branch_computations={%region_9.10_spmd, %region_10.11_spmd, %region_11.12_spmd, %region... | conditional | bytes 8257776
  70.6 1.8 %collective-permute-start.21 = (bf16[96,2432]{1,0:T(8,128)(2,1)S(1)}, bf16[96,2432]{1,0:T(8,128)(2,1)}, u32[]{:S(2)}, u32[]{:S(2)}) collective-permute-start(bf16[96,2432]{1,0:T(8,128)(2,1)S(1)} %get-tuple-element.98), channel_id=1, source_target_pairs={{0,1},{1,0},{2,3},{3,2},{4,5},{5,4},{6,7},{7,6},{8,9},{9,8},{10,11... | collective-permute-start | bytes 1400840 | tf_op jit(solution)/shard_map/cond/branch_3_fun/ppermute | solution.py:21
  77.2 5.3 %collective-permute-done.23 = bf16[24,7168]{1,0:T(8,128)(2,1)} collective-permute-done((bf16[24,7168]{1,0:T(8,128)(2,1)S(1)}, bf16[24,7168]{1,0:T(8,128)(2,1)}, u32[]{:S(2)}, u32[]{:S(2)}) %collective-permute-start.23) | collective-permute-done | bytes 344096 | tf_op jit(solution)/shard_map/cond/branch_3_fun/ppermute | solution.py:21
  82.5 3.7 %collective-permute-done.24 = bf16[24,7168]{1,0:T(8,128)(2,1)} collective-permute-done((bf16[24,7168]{1,0:T(8,128)(2,1)S(1)}, bf16[24,7168]{1,0:T(8,128)(2,1)}, u32[]{:S(2)}, u32[]{:S(2)}) %collective-permute-start.24) | collective-permute-done | bytes 344096 | tf_op jit(solution)/shard_map/cond/branch_3_fun/ppermute | solution.py:21
  86.2 2.5 %fusion.3 = (f32[1,24,7168]{2,1,0:T(8,128)}, f32[1,24,7168]{2,1,0:T(8,128)}) fusion(bf16[24,7168]{1,0:T(8,128)(2,1)} %get-tuple-element.185, pred[24]{0:T(512)(128)(4,1)S(1)} %iota_compare_fusion, pred[]{:T(512)S(6)} %ne.3, f32[24,2432]{1,0:T(8,128)S(1)} %convert_add_fusion, f32[24,2432]{1,0:T(8,128)S(1)} %convert_add_fusion.1, ...), kind=kLoop, calls=%fused_computation.9 | loop fusion | flops 2752512 | bytes 4128793 | tf_op jit(solution)/shard_map/broadcast_in_dim | solution.py:208
  88.8 4.0 %place.1 = bf16[128,7168]{1,0:T(8,128)(2,1)} custom-call(s32[3]{0:T(128)S(1)} %pad_add_fusion.1.refs_0_, s32[8,32]{1,0:T(8,128)S(1)} %bitcast.41, bf16[96,2304]{1,0:T(8,128)(2,1)S(1)} %pad_maximum_fusion.3.refs_2_, bf16[96,2432]{1,0:T(8,128)(2,1)S(1)} %get-tuple-element.196.refs_3_, bf16[96,2432]{1,0:T(8,128)(2,1)} %get-tuple-element.197.refs_4_, ...), custom_call_target="tpu_custom_call" | custom-call | tf_op jit(solution)/shard_map/place/pallas_call | solution.py:134
  (64 shorter events, 23.7 us)
Async XLA Ops:
  0.6 25.3 %copy-start.1 = (s32[32,8]{0,1:T(8,128)S(1)}, s32[32,8]{0,1:T(8,128)}, u32[]{:S(2)}) copy-start(s32[32,8]{0,1:T(8,128)} %param.20) | copy-start | bytes 3076
  4.6 32.6 %copy-start.2 = (f32[1,24,7168]{2,1,0:T(8,128)S(1)}, f32[1,24,7168]{2,1,0:T(8,128)}, u32[]{:S(2)}) copy-start(f32[1,24,7168]{2,1,0:T(8,128)} %param.19) | copy-start | bytes 2064388
  4.6 14.3 %collective-permute-start.31 = (bf16[96,2432]{1,0:T(8,128)(2,1)S(1)}, bf16[96,2432]{1,0:T(8,128)(2,1)S(1)}, u32[]{:S(2)}, u32[]{:S(2)}) collective-permute-start(bf16[96,2432]{1,0:T(8,128)(2,1)S(1)} %get-tuple-element.146), channel_id=1, source_target_pairs={{0,1},{1,0},{2,3},{3,2},{4,5},{5,4},{6,7},{7,6},{8,9},{9,8},{10,11... | collective-permute-start | bytes 1400840 | tf_op jit(solution)/shard_map/ppermute | solution.py:21
  6.9 11.9 %collective-permute-start.32 = (bf16[96,2432]{1,0:T(8,128)(2,1)S(1)}, bf16[96,2432]{1,0:T(8,128)(2,1)S(1)}, u32[]{:S(2)}, u32[]{:S(2)}) collective-permute-start(bf16[96,2432]{1,0:T(8,128)(2,1)S(1)} %get-tuple-element.147), channel_id=1, source_target_pairs={{0,3},{1,2},{2,1},{3,0},{4,7},{5,6},{6,5},{7,4},{8,11},{9,10},{10,... | collective-permute-start | bytes 1400840 | tf_op jit(solution)/shard_map/ppermute | solution.py:21
  7.3 11.5 %collective-permute-start.30 = (bf16[96,2304]{1,0:T(8,128)(2,1)S(1)}, bf16[96,2304]{1,0:T(8,128)(2,1)S(1)}, u32[]{:S(2)}, u32[]{:S(2)}) collective-permute-start(bf16[96,2304]{1,0:T(8,128)(2,1)S(1)} %get-tuple-element.145), channel_id=1, source_target_pairs={{0,4},{1,5},{2,6},{3,7},{4,0},{5,1},{6,2},{7,3},{8,12},{9,13},{10,... | collective-permute-start | bytes 1327112 | tf_op jit(solution)/shard_map/ppermute | solution.py:21
  19.2 10.6 %collective-permute-start.34 = (bf16[48,2432]{1,0:T(8,128)(2,1)S(1)}, bf16[48,2432]{1,0:T(8,128)(2,1)S(1)}, u32[]{:S(2)}, u32[]{:S(2)}) collective-permute-start(bf16[48,2432]{1,0:T(8,128)(2,1)S(1)} %get-tuple-element.152), channel_id=1, source_target_pairs={{0,3},{1,2},{2,1},{3,0},{4,7},{5,6},{6,5},{7,4},{8,11},{9,10},{10,... | collective-permute-start | bytes 700424 | tf_op jit(solution)/shard_map/ppermute | solution.py:21
  19.9 9.9 %collective-permute-start.35 = (bf16[48,2432]{1,0:T(8,128)(2,1)S(1)}, bf16[48,2432]{1,0:T(8,128)(2,1)S(1)}, u32[]{:S(2)}, u32[]{:S(2)}) collective-permute-start(bf16[48,2432]{1,0:T(8,128)(2,1)S(1)} %get-tuple-element.153), channel_id=1, source_target_pairs={{0,4},{1,5},{2,6},{3,7},{4,0},{5,1},{6,2},{7,3},{8,12},{9,13},{10,... | collective-permute-start | bytes 700424 | tf_op jit(solution)/shard_map/ppermute | solution.py:21
  23.2 6.6 %collective-permute-start.33 = (bf16[48,2304]{1,0:T(8,128)(2,1)S(1)}, bf16[48,2304]{1,0:T(8,128)(2,1)S(1)}, u32[]{:S(2)}, u32[]{:S(2)}) collective-permute-start(bf16[48,2304]{1,0:T(8,128)(2,1)S(1)} %get-tuple-element.151), channel_id=1, source_target_pairs={{0,1},{1,0},{2,3},{3,2},{4,5},{5,4},{6,7},{7,6},{8,9},{9,8},{10,11... | collective-permute-start | bytes 663560 | tf_op jit(solution)/shard_map/ppermute | solution.py:21
  29.9 4.8 %collective-permute-start.36 = (bf16[24,2304]{1,0:T(8,128)(2,1)S(1)}, bf16[24,2304]{1,0:T(8,128)(2,1)S(1)}, u32[]{:S(2)}, u32[]{:S(2)}) collective-permute-start(bf16[24,2304]{1,0:T(8,128)(2,1)S(1)} %get-tuple-element.155), channel_id=1, source_target_pairs={{0,3},{1,2},{2,1},{3,0},{4,7},{5,6},{6,5},{7,4},{8,11},{9,10},{10,... | collective-permute-start | bytes 331784 | tf_op jit(solution)/shard_map/ppermute | solution.py:21
  31.3 4.9 %collective-permute-start.37 = (bf16[24,2432]{1,0:T(8,128)(2,1)S(1)}, bf16[24,2432]{1,0:T(8,128)(2,1)S(1)}, u32[]{:S(2)}, u32[]{:S(2)}) collective-permute-start(bf16[24,2432]{1,0:T(8,128)(2,1)S(1)} %get-tuple-element.157), channel_id=1, source_target_pairs={{0,4},{1,5},{2,6},{3,7},{4,0},{5,1},{6,2},{7,3},{8,12},{9,13},{10,... | collective-permute-start | bytes 350216 | tf_op jit(solution)/shard_map/ppermute | solution.py:21
  31.7 5.4 %collective-permute-start.38 = (bf16[24,2432]{1,0:T(8,128)(2,1)S(1)}, bf16[24,2432]{1,0:T(8,128)(2,1)S(1)}, u32[]{:S(2)}, u32[]{:S(2)}) collective-permute-start(bf16[24,2432]{1,0:T(8,128)(2,1)S(1)} %get-tuple-element.159), channel_id=1, source_target_pairs={{0,1},{1,0},{2,3},{3,2},{4,5},{5,4},{6,7},{7,6},{8,9},{9,8},{10,11... | collective-permute-start | bytes 350216 | tf_op jit(solution)/shard_map/ppermute | solution.py:21
  38.7 7.6 %collective-permute-start.3 = (bf16[24,7168]{1,0:T(8,128)(2,1)}, bf16[24,7168]{1,0:T(8,128)(2,1)}, u32[]{:S(2)}, u32[]{:S(2)}) collective-permute-start(bf16[24,7168]{1,0:T(8,128)(2,1)} %param.3), channel_id=1, source_target_pairs={{0,64},{8,72},{16,80},{24,88},{32,96},{40,104},{48,112},{56,120},{... | collective-permute-start | bytes 1032200 | tf_op jit(solution)/shard_map/cond/branch_3_fun/ppermute | solution.py:21
  48.0 38.2 %copy-start.4 = (f32[1,24,7168]{2,1,0:T(8,128)S(1)}, f32[1,24,7168]{2,1,0:T(8,128)}, u32[]{:S(2)}) copy-start(f32[1,24,7168]{2,1,0:T(8,128)} %param.18) | copy-start | bytes 2064388
  49.2 9.5 %collective-permute-start.41 = (bf16[24,2432]{1,0:T(8,128)(2,1)S(1)}, bf16[24,2432]{1,0:T(8,128)(2,1)S(1)}, u32[]{:S(2)}, u32[]{:S(2)}) collective-permute-start(bf16[24,2432]{1,0:T(8,128)(2,1)S(1)} %get-tuple-element.194), channel_id=1, source_target_pairs={{0,1},{1,0},{2,3},{3,2},{4,5},{5,4},{6,7},{7,6},{8,9},{9,8},{10,11... | collective-permute-start | bytes 350216 | tf_op jit(solution)/shard_map/ppermute | solution.py:21
  51.3 7.4 %collective-permute-start.40 = (bf16[24,2432]{1,0:T(8,128)(2,1)S(1)}, bf16[24,2432]{1,0:T(8,128)(2,1)S(1)}, u32[]{:S(2)}, u32[]{:S(2)}) collective-permute-start(bf16[24,2432]{1,0:T(8,128)(2,1)S(1)} %get-tuple-element.195), channel_id=1, source_target_pairs={{0,4},{1,5},{2,6},{3,7},{4,0},{5,1},{6,2},{7,3},{8,12},{9,13},{10,... | collective-permute-start | bytes 350216 | tf_op jit(solution)/shard_map/ppermute | solution.py:21
  53.0 5.6 %collective-permute-start.39 = (bf16[24,2304]{1,0:T(8,128)(2,1)S(1)}, bf16[24,2304]{1,0:T(8,128)(2,1)S(1)}, u32[]{:S(2)}, u32[]{:S(2)}) collective-permute-start(bf16[24,2304]{1,0:T(8,128)(2,1)S(1)} %slice.12), channel_id=1, source_target_pairs={{0,3},{1,2},{2,1},{3,0},{4,7},{5,6},{6,5},{7,4},{8,11},{9,10},{10,... | collective-permute-start | bytes 331784 | tf_op jit(solution)/shard_map/ppermute | solution.py:21
  58.7 8.4 %collective-permute-start.42 = (bf16[48,2304]{1,0:T(8,128)(2,1)S(1)}, bf16[48,2304]{1,0:T(8,128)(2,1)S(1)}, u32[]{:S(2)}, u32[]{:S(2)}) collective-permute-start(bf16[48,2304]{1,0:T(8,128)(2,1)S(1)} %pad_maximum_fusion.6), channel_id=1, source_target_pairs={{0,1},{1,0},{2,3},{3,2},{4,5},{5,4},{6,7},{7,6},{8,9},{9,8},{10,11... | collective-permute-start | bytes 663560 | tf_op jit(solution)/shard_map/ppermute | solution.py:21
  60.3 8.4 %collective-permute-start.44 = (bf16[48,2432]{1,0:T(8,128)(2,1)S(1)}, bf16[48,2432]{1,0:T(8,128)(2,1)S(1)}, u32[]{:S(2)}, u32[]{:S(2)}) collective-permute-start(bf16[48,2432]{1,0:T(8,128)(2,1)S(1)} %pad_maximum_fusion.5), channel_id=1, source_target_pairs={{0,4},{1,5},{2,6},{3,7},{4,0},{5,1},{6,2},{7,3},{8,12},{9,13},{10,... | collective-permute-start | bytes 700424 | tf_op jit(solution)/shard_map/ppermute | solution.py:21
  61.1 8.6 %collective-permute-start.43 = (bf16[48,2432]{1,0:T(8,128)(2,1)S(1)}, bf16[48,2432]{1,0:T(8,128)(2,1)S(1)}, u32[]{:S(2)}, u32[]{:S(2)}) collective-permute-start(bf16[48,2432]{1,0:T(8,128)(2,1)S(1)} %pad_maximum_fusion.4), channel_id=1, source_target_pairs={{0,3},{1,2},{2,1},{3,0},{4,7},{5,6},{6,5},{7,4},{8,11},{9,10},{10,... | collective-permute-start | bytes 700424 | tf_op jit(solution)/shard_map/ppermute | solution.py:21
  70.6 15.6 %collective-permute-start.21 = (bf16[96,2432]{1,0:T(8,128)(2,1)S(1)}, bf16[96,2432]{1,0:T(8,128)(2,1)}, u32[]{:S(2)}, u32[]{:S(2)}) collective-permute-start(bf16[96,2432]{1,0:T(8,128)(2,1)S(1)} %get-tuple-element.98), channel_id=1, source_target_pairs={{0,1},{1,0},{2,3},{3,2},{4,5},{5,4},{6,7},{7,6},{8,9},{9,8},{10,11... | collective-permute-start | bytes 1400840 | tf_op jit(solution)/shard_map/cond/branch_3_fun/ppermute | solution.py:21
  72.4 13.8 %collective-permute-start.22 = (bf16[96,2432]{1,0:T(8,128)(2,1)}, bf16[96,2432]{1,0:T(8,128)(2,1)}, u32[]{:S(2)}, u32[]{:S(2)}) collective-permute-start(bf16[96,2432]{1,0:T(8,128)(2,1)} %get-tuple-element.99), channel_id=1, source_target_pairs={{0,3},{1,2},{2,1},{3,0},{4,7},{5,6},{6,5},{7,4},{8,11},{9,10},{10,... | collective-permute-start | bytes 1400840 | tf_op jit(solution)/shard_map/cond/branch_3_fun/ppermute | solution.py:21
  73.7 12.5 %collective-permute-start.20 = (bf16[96,2304]{1,0:T(8,128)(2,1)S(1)}, bf16[96,2304]{1,0:T(8,128)(2,1)}, u32[]{:S(2)}, u32[]{:S(2)}) collective-permute-start(bf16[96,2304]{1,0:T(8,128)(2,1)S(1)} %get-tuple-element.97), channel_id=1, source_target_pairs={{0,4},{1,5},{2,6},{3,7},{4,0},{5,1},{6,2},{7,3},{8,12},{9,13},{10,... | collective-permute-start | bytes 1327112 | tf_op jit(solution)/shard_map/cond/branch_3_fun/ppermute | solution.py:21
  75.2 7.4 %collective-permute-start.23 = (bf16[24,7168]{1,0:T(8,128)(2,1)S(1)}, bf16[24,7168]{1,0:T(8,128)(2,1)}, u32[]{:S(2)}, u32[]{:S(2)}) collective-permute-start(bf16[24,7168]{1,0:T(8,128)(2,1)S(1)} %get-tuple-element.100), channel_id=1, source_target_pairs={{0,64},{8,72},{16,80},{24,88},{32,96},{40,104},{48,112},{56,120},{... | collective-permute-start | bytes 1032200 | tf_op jit(solution)/shard_map/cond/branch_3_fun/ppermute | solution.py:21
  76.8 9.5 %collective-permute-start.24 = (bf16[24,7168]{1,0:T(8,128)(2,1)S(1)}, bf16[24,7168]{1,0:T(8,128)(2,1)}, u32[]{:S(2)}, u32[]{:S(2)}) collective-permute-start(bf16[24,7168]{1,0:T(8,128)(2,1)S(1)} %get-tuple-element.101), channel_id=1, source_target_pairs={{0,64},{8,72},{16,80},{24,88},{32,96},{40,104},{48,112},{56,120},{... | collective-permute-start | bytes 1032200 | tf_op jit(solution)/shard_map/cond/branch_3_fun/ppermute | solution.py:21
  (6 other events, 82.4 us)
where the time goes:
time: 93.4 us; the launch traced here: 92.7 us
  waiting for transfers between devices  38.5 us (41%)
  starting transfers between devices  31 us (33%)
  other arithmetic  11 us (12%)
  Pallas kernels  7.5 us (8%)
  local copies, waits for them, and re-layouts  2.51 us (3%)
  between operations  2.15 us (2%)
    ppermute x21, waiting for transfers between devices, flipped_by(): lax.ppermute(array, axis, [(i, i ^ mask) for i in range(lax.axis_size(axi...  38.5 us
    ppermute x21, starting transfers between devices, flipped_by(): lax.ppermute(array, axis, [(i, i ^ mask) for i in range(lax.axis_size(axi...  31 us
    broadcast_in_dim x2, other arithmetic, body(): jnp.where(moves, arrived.astype(jnp.float32), own)[None]  4.41 us
    pallas_call x1, Pallas kernels, place(): pl.pallas_call(lambda *refs: place_kernel(cuts, capacity, *refs), in_spec...  3.96 us
    pallas_call x1, Pallas kernels, pack(): pl.pallas_call(lambda *refs: pack_kernel(cuts, capacity, *refs), in_specs...  3.13 us
    unnamed x19, local copies, waits for them, and re-layouts  2.49 us
  transfers between devices with their start and end apart: 21, of which 12 were waited for; matrix products, arithmetic and copies ran while one was open for 5% of the time, Pallas kernels for 0%

commit v1 on v0

--- a/solution.py
+++ b/solution.py
@@ -92,52 +92,83 @@
     )(where, rows_by_shard, gradients)
 
 
-def sum_kernel(*refs):
-    kept, arrived, outs = refs[:3], refs[3:6], refs[6:]
-    rest = kept[0].shape[0] // 2
+def sum_kernel(kept_ref, arrived_ref, sent_ref, next_ref):
+    rest = next_ref.shape[0]
+    sent_ref[...] = (
+        kept_ref[rest:].astype(jnp.float32) + arrived_ref[rest:].astype(jnp.float32)
+    ).astype(jnp.bfloat16)
+    next_ref[...] = kept_ref[:rest].astype(jnp.float32) + arrived_ref[:rest].astype(jnp.float32)
+
+
+def summed(kept, arrived):
+    shape = (kept.shape[0] // 2, kept.shape[1])
+    return pl.pallas_call(
+        sum_kernel,
+        in_specs=[vmem_spec] * 2,
+        out_specs=[vmem_spec] * 2,
+        out_shape=[jax.ShapeDtypeStruct(shape, jnp.bfloat16), jax.ShapeDtypeStruct(shape, jnp.float32)],
+        compiler_params=params,
+        name="sums",
+    )(kept, arrived)
+
+
+def join_kernel(here_ref, arrived_ref, out_ref):
+    rows = here_ref.shape[0]
+    out_ref[:rows] = here_ref[...]
+    out_ref[rows:] = arrived_ref[...]
+
+
+def joined(here, arrived):
+    return pl.pallas_call(
+        join_kernel,
+        in_specs=[vmem_spec] * 2,
+        out_specs=vmem_spec,
+        out_shape=jax.ShapeDtypeStruct((2 * here.shape[0], here.shape[1]), jnp.bfloat16),
+        compiler_params=params,
+        name="join",
+    )(here, arrived)
+
+
+def finish_kernel(cuts, capacity, place_ref, rows_ref, *refs):
+    here, arrived, moved, own = refs[:3], refs[3:6], refs[6:8], refs[8:10]
+    placed_ref, moment_refs = refs[10], refs[11:13]
+    rows_out, moments_out, sems = refs[13:]
+    moves = place_ref[2] != place_ref[0]
+    copies = []
+    for m in range(2):
+        moments_out[m] = jnp.where(moves, moved[m][...].astype(jnp.float32), own[m][...])
+        copies.append(pltpu.make_async_copy(moments_out.at[m], moment_refs[m].at[0], sems.at[m]))
+        copies[-1].start()
     for g in range(3):
-        outs[g][...] = (
-            kept[g][rest:].astype(jnp.float32) + arrived[g][rest:].astype(jnp.float32)
-        ).astype(jnp.bfloat16)
-        outs[3 + g][...] = kept[g][:rest].astype(jnp.float32) + arrived[g][:rest].astype(jnp.float32)
-
-
-def summed(kept, arrived):
-    shapes = [
-        jax.ShapeDtypeStruct((k.shape[0] // 2, k.shape[1]), dtype)
-        for dtype in (jnp.bfloat16, jnp.float32)
-        for k in kept
-    ]
-    outs = pl.pallas_call(
-        sum_kernel,
-        in_specs=[vmem_spec] * 6,
-        out_specs=[vmem_spec] * 6,
-        out_shape=shapes,
-        compiler_params=params,
-        name="sums",
-    )(*kept, *arrived)
-    return outs[:3], outs[3:]
-
-
-def place_kernel(cuts, capacity, place_ref, rows_ref, *refs):
-    here, arrived, out_ref = refs[:3], refs[3:6], refs[6]
-    half = 4 * capacity
-    for g in range(3):
-        hot = slots_to_rows(rows_ref, place_ref[2], place_ref[1], orders[g], capacity, out_ref.shape[0])
+        part = pl.ds(cuts[g], cuts[g + 1] - cuts[g])
+        hot = slots_to_rows(rows_ref, place_ref[2], place_ref[1], orders[g], capacity, rows_out.shape[0])
         hot = hot.T.astype(jnp.bfloat16)
-        total = jnp.dot(hot[:, :half], here[g][...], preferred_element_type=jnp.float32)
-        total += jnp.dot(hot[:, half:], arrived[g][...], preferred_element_type=jnp.float32)
-        out_ref[:, cuts[g] : cuts[g + 1]] = total.astype(jnp.bfloat16)
-
-
-def place(where, rows_by_shard, here, arrived, cuts, capacity, flat_count):
-    return pl.pallas_call(
-        lambda *refs: place_kernel(cuts, capacity, *refs),
-        in_specs=[smem_spec, smem_spec] + [vmem_spec] * 6,
-        out_shape=jax.ShapeDtypeStruct((flat_count, cuts[-1]), jnp.bfloat16),
-        compiler_params=params,
-        name="place",
-    )(where, rows_by_shard, *here, *arrived)
+        rows = jnp.concatenate([here[g][...], arrived[g][...]], axis=0)
+        total = jnp.dot(hot, rows, preferred_element_type=jnp.float32)
+        rows_out[:, cuts[g] : cuts[g + 1]] = total.astype(jnp.bfloat16)
+        copies.append(pltpu.make_async_copy(rows_out.at[:, part], placed_ref.at[:, part], sems.at[2 + g]))
+        copies[-1].start()
+    for copy in copies:
+        copy.wait()
+
+
+def finished(where, rows_by_shard, here, arrived, moved, own, cuts, flat_count):
+    capacity, width = own[0].shape
+    hbm_spec = pl.BlockSpec(memory_space=pltpu.HBM)
+    moment = jax.ShapeDtypeStruct((1, capacity, width), jnp.float32)
+    return pl.pallas_call(
+        lambda *refs: finish_kernel(cuts, capacity, *refs),
+        in_specs=[smem_spec, smem_spec] + [vmem_spec] * 10,
+        out_specs=[hbm_spec] * 3,
+        out_shape=[jax.ShapeDtypeStruct((flat_count, width), jnp.bfloat16), moment, moment],
+        scratch_shapes=[
+            pltpu.VMEM((flat_count, width), jnp.bfloat16),
+            pltpu.VMEM((2, capacity, width), jnp.float32),
+            pltpu.SemaphoreType.DMA((5,)),
+        ],
+        compiler_params=params,
+        name="finish",
+    )(where, rows_by_shard, *here, *arrived, *moved, *own)
 
 
 def body(gradients, master_rows, first_moment, second_moment, shard_rows, move_partner):
@@ -152,12 +183,15 @@
 
     rows_by_shard = shard_rows.T
     packed = pack(where, rows_by_shard, gradients, cuts, capacity)
-    sent, kept = packed[:3], packed[3:]
-    for step in range(3):
-        arrived = [flipped_by(sent[g], "dp", orders[g][step]) for g in range(3)]
-        if step < 2:
-            sent, kept = summed(kept, arrived)
-    grad_own = jnp.concatenate([k + a.astype(jnp.float32) for k, a in zip(kept, arrived)], axis=1) / 8
+    grads = []
+    for g, order in enumerate(orders):
+        sent, kept = packed[g], packed[3 + g]
+        for step in range(3):
+            arrived = flipped_by(sent, "dp", order[step])
+            if step < 2:
+                sent, kept = summed(kept, arrived)
+        grads.append(kept + arrived.astype(jnp.float32))
+    grad_own = jnp.concatenate(grads, axis=1) / 8
 
     partner = jnp.sum(jnp.where(ep_all == ep_index, move_partner, 0))
     own_counts = jnp.sum(jnp.where((ep_all == ep_index)[:, None], shard_rows, 0), axis=0)
@@ -168,46 +202,42 @@
     bits = move_partner.shape[0].bit_length() - 1
     which_bit = jnp.max(sum((flips >= 1 << b).astype(jnp.int32) for b in range(1, bits)))
 
+    sent_master = adam_step(grad_own, master_rows[0], first_moment[0], second_moment[0], live)[0]
+    sent_master = sent_master.astype(jnp.bfloat16)
+    (there,) = lax.switch(
+        which_bit,
+        [lambda o, b=b: [flipped_by(a, "ep", 1 << b) for a in o] for b in range(bits)],
+        [sent_master],
+    )
+    narrow = jnp.where(moves, there, sent_master)
+    here = [narrow[:, cuts[g] : cuts[g + 1]] for g in range(3)]
+    here = [joined(h, flipped_by(h, "dp", order[2])) for h, order in zip(here, orders)]
+    here, grad_own = lax.optimization_barrier((here, grad_own))
     updated, first_new, second_new = adam_step(
         grad_own, master_rows[0], first_moment[0], second_moment[0], live
     )
-
-    def relocated(apart, arrays):
-        return [flipped_by(a, "ep", 1 << apart) for a in arrays]
-
-    sent_master = updated.astype(jnp.bfloat16)
-    (there,) = lax.switch(
-        which_bit, [lambda o, b=b: relocated(b, o) for b in range(bits)], [sent_master]
-    )
-    narrow = jnp.where(moves, there, sent_master)
-    here = [narrow[:, cuts[g] : cuts[g + 1]] for g in range(3)]
-    for step in range(2):
-        arrived = [flipped_by(here[g], "dp", orders[g][2 - step]) for g in range(3)]
-        arrived = lax.optimization_barrier(arrived)
-        here = [jnp.concatenate(pair, axis=0) for pair in zip(here, arrived)]
+    here = [joined(h, flipped_by(h, "dp", order[1])) for h, order in zip(here, orders)]
 
     def last(apart, operands):
         here, moments = operands
         arrived = [flipped_by(here[g], "dp", orders[g][0]) for g in range(3)]
-        return arrived, relocated(apart, moments)
+        return arrived, [flipped_by(m, "ep", 1 << apart) for m in moments]
 
     moments = [first_new.astype(jnp.bfloat16), second_new.astype(jnp.bfloat16)]
     arrived, moments = lax.switch(
         which_bit, [lambda o, b=b: last(b, o) for b in range(bits)], (here, moments)
     )
-    placed = place(
+    placed, new_first, new_second = finished(
         jnp.stack([ep_index, dp_index, partner]).astype(jnp.int32),
         rows_by_shard,
         here,
         arrived,
+        moments,
+        (first_new, second_new),
         cuts,
-        capacity,
         flat_count,
     )
-    new_master, new_first, new_second = [
-        jnp.where(moves, arrived.astype(jnp.float32), own)[None]
-        for arrived, own in ((there, updated), (moments[0], first_new), (moments[1], second_new))
-    ]
+    new_master = jnp.where(moves, narrow.astype(jnp.float32), updated)[None]
     return new_master, new_first, new_second, placed
 
 

time: 93.4 us -> 120 us (1.28)
  waiting for transfers between devices: 38.5 us -> 63.7 us
  starting transfers between devices: 31 us -> 36.9 us
  other arithmetic: 11 us -> 8.01 us
  local copies, waits for them, and re-layouts: 2.51 us -> 0.75 us
    ppermute x21, waiting for transfers between devices: 38.5 us -> 63.7 us  [flipped_by(): lax.ppermute(array, axis, [(i, i ^ mask) for i in range(lax.axis_size(axi...]
    ppermute x21, starting transfers between devices: 31 us -> 36.9 us  [flipped_by(): lax.ppermute(array, axis, [(i, i ^ mask) for i in range(lax.axis_size(axi...]
    broadcast_in_dim x2 -> x0, other arithmetic: 4.41 us -> none  [body(): jnp.where(moves, arrived.astype(jnp.float32), own)[None]]
    unnamed x19 -> x16, local copies, waits for them, and re-layouts: 2.49 us -> 0.72 us
    div x0 -> x1, other arithmetic: none -> 1.41 us  [body(): grad_own = jnp.concatenate(grads, axis=1) / 8]
    pallas_call x3 -> x13, Pallas kernels: 4.37 us -> 4.29 us  [the longest x1 3.72 us: finished(): pl.pallas_call(lambda *refs: finish_kernel(cuts, capacity, *refs), in_spe...]
  transfers between devices with their start and end apart: 21 -> 21, of which waited for: 12 -> 11; matrix products, arithmetic and copies ran while one was open for 5% -> 5% of each run, Pallas kernels for 0% -> 0%
where the time goes in v1:
time: 120 us; the launch traced here: 119 us
  waiting for transfers between devices  63.7 us (53%)
  starting transfers between devices  36.9 us (31%)
  other arithmetic  8.01 us (7%)
  Pallas kernels  7.42 us (6%)
  between operations  2.3 us (2%)
    ppermute x21, waiting for transfers between devices, flipped_by(): lax.ppermute(array, axis, [(i, i ^ mask) for i in range(lax.axis_size(axi...  63.7 us
    ppermute x21, starting transfers between devices, flipped_by(): lax.ppermute(array, axis, [(i, i ^ mask) for i in range(lax.axis_size(axi...  36.9 us
    pallas_call x1, Pallas kernels, finished(): pl.pallas_call(lambda *refs: finish_kernel(cuts, capacity, *refs), in_spe...  3.72 us
    pallas_call x1, Pallas kernels, pack(): pl.pallas_call(lambda *refs: pack_kernel(cuts, capacity, *refs), in_specs...  3.13 us
    convert_element_type x1, other arithmetic, body(): moments = [first_new.astype(jnp.bfloat16), second_new.astype(jnp.bfloat16)]  2.65 us
  transfers between devices with their start and end apart: 21, of which 11 were waited for; matrix products, arithmetic and copies ran while one was open for 5% of the time, Pallas kernels for 0%

profile of v1, /device:TPU:2, one launch (start us, length us, event | category | flops | bytes accessed | tf_op | source)
XLA Modules:
  0.0 119.1 jit_solution(11435740775211772415)
XLA Ops:
  1.4 3.1 %pack.1 = (bf16[96,2304]{1,0:T(8,128)(2,1)S(1)}, bf16[96,2432]{1,0:T(8,128)(2,1)S(1)}, bf16[96,2432]{1,0:T(8,128)(2,1)S(1)}, bf16[96,2304]{1,0:T(8,128)(2,1)S(1)...) custom-call(s32[2]{0:T(128)S(1)} %pad_add_fusion.refs_0_, s32[8,32]{1,0:T(8,128)S(1)} %bitcast.64, ...), custom_call_target="tpu_custom_call" | custom-call | tf_op jit(solution)/shard_map/pack/pallas_call | solution.py:84
  4.6 2.4 %collective-permute-start.33 = (bf16[96,2432]{1,0:T(8,128)(2,1)S(1)}, bf16[96,2432]{1,0:T(8,128)(2,1)S(1)}, u32[]{:S(2)}, u32[]{:S(2)}) collective-permute-start(bf16[96,2432]{1,0:T(8,128)(2,1)S(1)} %get-tuple-element.127), channel_id=1, source_target_pairs={{0,1},{1,0},{2,3},{3,2},{4,5},{5,4},{6,7},{7,6},{8,9},{9,8},{10,11... | collective-permute-start | bytes 1400840 | tf_op jit(solution)/shard_map/ppermute | solution.py:21
  7.3 1.9 %collective-permute-start.30 = (bf16[96,2304]{1,0:T(8,128)(2,1)S(1)}, bf16[96,2304]{1,0:T(8,128)(2,1)S(1)}, u32[]{:S(2)}, u32[]{:S(2)}) collective-permute-start(bf16[96,2304]{1,0:T(8,128)(2,1)S(1)} %get-tuple-element.121), channel_id=1, source_target_pairs={{0,4},{1,5},{2,6},{3,7},{4,0},{5,1},{6,2},{7,3},{8,12},{9,13},{10,... | collective-permute-start | bytes 1327112 | tf_op jit(solution)/shard_map/ppermute | solution.py:21
  9.9 9.0 %collective-permute-done.30.arrived_ref = bf16[96,2304]{1,0:T(8,128)(2,1)S(1)} collective-permute-done((bf16[96,2304]{1,0:T(8,128)(2,1)S(1)}, bf16[96,2304]{1,0:T(8,128)(2,1)S(1)}, u32[]{:S(2)}, u32[]{:S(2)}) %collective-permute-start.30) | collective-permute-done | bytes 442400 | tf_op jit(solution)/shard_map/ppermute | solution.py:21
  21.3 1.8 %collective-permute-start.37 = (bf16[48,2432]{1,0:T(8,128)(2,1)S(1)}, bf16[48,2432]{1,0:T(8,128)(2,1)S(1)}, u32[]{:S(2)}, u32[]{:S(2)}) collective-permute-start(bf16[48,2432]{1,0:T(8,128)(2,1)S(1)} %get-tuple-element.135), channel_id=1, source_target_pairs={{0,4},{1,5},{2,6},{3,7},{4,0},{5,1},{6,2},{7,3},{8,12},{9,13},{10,... | collective-permute-start | bytes 700424 | tf_op jit(solution)/shard_map/ppermute | solution.py:21
  25.3 1.6 %collective-permute-start.32 = (bf16[24,2304]{1,0:T(8,128)(2,1)S(1)}, bf16[24,2304]{1,0:T(8,128)(2,1)S(1)}, u32[]{:S(2)}, u32[]{:S(2)}) collective-permute-start(bf16[24,2304]{1,0:T(8,128)(2,1)S(1)} %get-tuple-element.125), channel_id=1, source_target_pairs={{0,3},{1,2},{2,1},{3,0},{4,7},{5,6},{6,5},{7,4},{8,11},{9,10},{10,... | collective-permute-start | bytes 331784 | tf_op jit(solution)/shard_map/ppermute | solution.py:21
  28.0 1.8 %collective-permute-start.35 = (bf16[24,2432]{1,0:T(8,128)(2,1)S(1)}, bf16[24,2432]{1,0:T(8,128)(2,1)S(1)}, u32[]{:S(2)}, u32[]{:S(2)}) collective-permute-start(bf16[24,2432]{1,0:T(8,128)(2,1)S(1)} %get-tuple-element.131), channel_id=1, source_target_pairs={{0,4},{1,5},{2,6},{3,7},{4,0},{5,1},{6,2},{7,3},{8,12},{9,13},{10,... | collective-permute-start | bytes 350216 | tf_op jit(solution)/shard_map/ppermute | solution.py:21
  29.9 1.7 %collective-permute-start.38 = (bf16[24,2432]{1,0:T(8,128)(2,1)S(1)}, bf16[24,2432]{1,0:T(8,128)(2,1)S(1)}, u32[]{:S(2)}, u32[]{:S(2)}) collective-permute-start(bf16[24,2432]{1,0:T(8,128)(2,1)S(1)} %get-tuple-element.137), channel_id=1, source_target_pairs={{0,1},{1,0},{2,3},{3,2},{4,5},{5,4},{6,7},{7,6},{8,9},{9,8},{10,11... | collective-permute-start | bytes 350216 | tf_op jit(solution)/shard_map/ppermute | solution.py:21
  32.9 1.9 %collective-permute-done.38 = bf16[24,2432]{1,0:T(8,128)(2,1)S(1)} collective-permute-done((bf16[24,2432]{1,0:T(8,128)(2,1)S(1)}, bf16[24,2432]{1,0:T(8,128)(2,1)S(1)}, u32[]{:S(2)}, u32[]{:S(2)}) %collective-permute-start.38) | collective-permute-done | bytes 116768 | tf_op jit(solution)/shard_map/ppermute | solution.py:21
  36.2 16.4 %conditional.2 = (bf16[24,7168]{1,0:T(8,128)(2,1)}) conditional(s32[]{:T(128)} %clamp.4, bf16[24,7168]{1,0:T(8,128)(2,1)S(1)} %get-tuple-element.160, bf16[24,7168]{1,0:T(8,128)(2,1)S(1)} %get-tuple-element.160, bf16[24,7168]{1,0:T(8,128)(2,1)S(1)} %get-tuple-element.160, ...), branch_computations={%region_4.5_spmd, %region_5.6_spmd, %region_6.7_spmd, %region_7.8_... | conditional | bytes 1376304 | solution.py:207
  36.2 6.3 %collective-permute-start.2 = (bf16[24,7168]{1,0:T(8,128)(2,1)S(1)}, bf16[24,7168]{1,0:T(8,128)(2,1)}, u32[]{:S(2)}, u32[]{:S(2)}) collective-permute-start(bf16[24,7168]{1,0:T(8,128)(2,1)S(1)} %param.2), channel_id=1, source_target_pairs={{0,32},{8,40},{16,48},{24,56},{32,0},{40,8},{48,16},{56,24},{64,96... | collective-permute-start | bytes 1032200 | tf_op jit(solution)/shard_map/cond/branch_2_fun/ppermute | solution.py:21
  42.5 10.1 %collective-permute-done.2 = bf16[24,7168]{1,0:T(8,128)(2,1)} collective-permute-done((bf16[24,7168]{1,0:T(8,128)(2,1)S(1)}, bf16[24,7168]{1,0:T(8,128)(2,1)}, u32[]{:S(2)}, u32[]{:S(2)}) %collective-permute-start.2) | collective-permute-done | bytes 344096 | tf_op jit(solution)/shard_map/cond/branch_2_fun/ppermute | solution.py:21
  55.0 2.5 %collective-permute-start.40 = (bf16[24,2432]{1,0:T(8,128)(2,1)S(1)}, bf16[24,2432]{1,0:T(8,128)(2,1)S(1)}, u32[]{:S(2)}, u32[]{:S(2)}) collective-permute-start(bf16[24,2432]{1,0:T(8,128)(2,1)S(1)} %get-tuple-element.162.here_ref), channel_id=1, source_target_pairs={{0,4},{1,5},{2,6},{3,7},{4,0},{5,1},{6,2},{7,3},{8,12},{9,13},{10,... | collective-permute-start | bytes 350216 | tf_op jit(solution)/shard_map/ppermute | solution.py:21
  58.9 4.4 %collective-permute-done.39.arrived_ref = bf16[24,2304]{1,0:T(8,128)(2,1)S(1)} collective-permute-done((bf16[24,2304]{1,0:T(8,128)(2,1)S(1)}, bf16[24,2304]{1,0:T(8,128)(2,1)S(1)}, u32[]{:S(2)}, u32[]{:S(2)}) %collective-permute-start.39) | collective-permute-done | bytes 110624 | tf_op jit(solution)/shard_map/ppermute | solution.py:21
  63.4 1.6 %collective-permute-start.42 = (bf16[48,2304]{1,0:T(8,128)(2,1)S(1)}, bf16[48,2304]{1,0:T(8,128)(2,1)S(1)}, u32[]{:S(2)}, u32[]{:S(2)}) collective-permute-start(bf16[48,2304]{1,0:T(8,128)(2,1)S(1)} %join.6.here_ref), channel_id=1, source_target_pairs={{0,1},{1,0},{2,3},{3,2},{4,5},{5,4},{6,7},{7,6},{8,9},{9,8},{10,11... | collective-permute-start | bytes 663560 | tf_op jit(solution)/shard_map/ppermute | solution.py:21
  66.2 2.7 %fusion.20 = (bf16[24,7168]{1,0:T(8,128)(2,1)S(1)}, f32[24,7168]{1,0:T(8,128)S(1)}, f32[1,24,7168]{2,1,0:T(8,128)}, bf16[24,7168]{1,0:T(8,128)(2,1)S(1)}, f32[24,7168]{1,0:T(8,128)S(1)}) fusion(f32[24,7168]{1,0:T(8,128)} %get-tuple-element.138, f32[1,24,7168]{2,1,0:T(8,128)S(1)} %copy-done.2, pred[24]{0:T(512)(128)(4,1)S(1)} %iota_compare_fusion, ...), kind=kLoop, calls=%fused_computation.45 | loop fusion | flops 3784704 | bytes 5849113 | tf_op jit(solution)/shard_map/convert_element_type | solution.py:226
  68.8 2.4 %collective-permute-done.42.arrived_ref = bf16[48,2304]{1,0:T(8,128)(2,1)S(1)} collective-permute-done((bf16[48,2304]{1,0:T(8,128)(2,1)S(1)}, bf16[48,2304]{1,0:T(8,128)(2,1)S(1)}, u32[]{:S(2)}, u32[]{:S(2)}) %collective-permute-start.42) | collective-permute-done | bytes 221216 | tf_op jit(solution)/shard_map/ppermute | solution.py:21
  71.3 1.8 %collective-permute-done.43.arrived_ref = bf16[48,2432]{1,0:T(8,128)(2,1)S(1)} collective-permute-done((bf16[48,2432]{1,0:T(8,128)(2,1)S(1)}, bf16[48,2432]{1,0:T(8,128)(2,1)S(1)}, u32[]{:S(2)}, u32[]{:S(2)}) %collective-permute-start.43) | collective-permute-done | bytes 233504 | tf_op jit(solution)/shard_map/ppermute | solution.py:21
  73.7 41.5 %conditional.3 = (bf16[96,2304]{1,0:T(8,128)(2,1)}, bf16[96,2432]{1,0:T(8,128)(2,1)}, bf16[96,2432]{1,0:T(8,128)(2,1)}, bf16[24,7168]{1,0:T(8,128)(2,1)}, bf16[24,7168]{1,0:T(8,128)(2,1)}) conditional(s32[]{:T(128)} %clamp.4, (bf16[96,2304]{1,0:T(8,128)(2,1)S(1)}, bf16[96,2432]{1,0:T(8,128)(2,1)S(1)}, ...), branch_computations={%region_9.10_spmd, %region_10.11_spmd, %region_11.12_spmd, %region... | conditional | bytes 8257776 | solution.py:227
  75.2 1.6 %collective-permute-start.17 = (bf16[96,2432]{1,0:T(8,128)(2,1)S(1)}, bf16[96,2432]{1,0:T(8,128)(2,1)}, u32[]{:S(2)}, u32[]{:S(2)}) collective-permute-start(bf16[96,2432]{1,0:T(8,128)(2,1)S(1)} %get-tuple-element.73), channel_id=1, source_target_pairs={{0,3},{1,2},{2,1},{3,0},{4,7},{5,6},{6,5},{7,4},{8,11},{9,10},{10,... | collective-permute-start | bytes 1400840 | tf_op jit(solution)/shard_map/cond/branch_2_fun/ppermute | solution.py:21
  76.8 6.6 %collective-permute-start.18 = (bf16[24,7168]{1,0:T(8,128)(2,1)S(1)}, bf16[24,7168]{1,0:T(8,128)(2,1)}, u32[]{:S(2)}, u32[]{:S(2)}) collective-permute-start(bf16[24,7168]{1,0:T(8,128)(2,1)S(1)} %get-tuple-element.74), channel_id=1, source_target_pairs={{0,32},{8,40},{16,48},{24,56},{32,0},{40,8},{48,16},{56,24},{64,96... | collective-permute-start | bytes 1032200 | tf_op jit(solution)/shard_map/cond/branch_2_fun/ppermute | solution.py:21
  83.4 20.3 %collective-permute-done.18 = bf16[24,7168]{1,0:T(8,128)(2,1)} collective-permute-done((bf16[24,7168]{1,0:T(8,128)(2,1)S(1)}, bf16[24,7168]{1,0:T(8,128)(2,1)}, u32[]{:S(2)}, u32[]{:S(2)}) %collective-permute-start.18) | collective-permute-done | bytes 344096 | tf_op jit(solution)/shard_map/cond/branch_2_fun/ppermute | solution.py:21
  103.7 11.6 %collective-permute-done.19 = bf16[24,7168]{1,0:T(8,128)(2,1)} collective-permute-done((bf16[24,7168]{1,0:T(8,128)(2,1)S(1)}, bf16[24,7168]{1,0:T(8,128)(2,1)}, u32[]{:S(2)}, u32[]{:S(2)}) %collective-permute-start.19) | collective-permute-done | bytes 344096 | tf_op jit(solution)/shard_map/cond/branch_2_fun/ppermute | solution.py:21
  115.2 3.7 %finish.1 = (bf16[128,7168]{1,0:T(8,128)(2,1)}, f32[1,24,7168]{2,1,0:T(8,128)}, f32[1,24,7168]{2,1,0:T(8,128)}) custom-call(s32[3]{0:T(128)S(1)} %pad_add_fusion.1.refs_0_, s32[8,32]{1,0:T(8,128)S(1)} %bitcast.65, bf16[96,2304]{1,0:T(8,128)(2,1)S(1)} %join.9.refs_2_, bf16[96,2432]{1,0:T(8,128)(2,1)S(1)} %join.10.refs_3_, bf16[96,2432]{1,0:T(8,128)(2,1)S(1)} %join.11.refs_4_, ...), custom_call_target="tpu_custom_call" | custom-call | tf_op jit(solution)/shard_map/finish/pallas_call | solution.py:159
  (65 shorter events, 16.3 us)
Async XLA Ops:
  4.6 30.2 %copy-start.2 = (f32[1,24,7168]{2,1,0:T(8,128)S(1)}, f32[1,24,7168]{2,1,0:T(8,128)}, u32[]{:S(2)}) copy-start(f32[1,24,7168]{2,1,0:T(8,128)} %param.19) | copy-start | bytes 2064388
  4.6 15.9 %collective-permute-start.33 = (bf16[96,2432]{1,0:T(8,128)(2,1)S(1)}, bf16[96,2432]{1,0:T(8,128)(2,1)S(1)}, u32[]{:S(2)}, u32[]{:S(2)}) collective-permute-start(bf16[96,2432]{1,0:T(8,128)(2,1)S(1)} %get-tuple-element.127), channel_id=1, source_target_pairs={{0,1},{1,0},{2,3},{3,2},{4,5},{5,4},{6,7},{7,6},{8,9},{9,8},{10,11... | collective-permute-start | bytes 1400840 | tf_op jit(solution)/shard_map/ppermute | solution.py:21
  6.9 14.3 %collective-permute-start.36 = (bf16[96,2432]{1,0:T(8,128)(2,1)S(1)}, bf16[96,2432]{1,0:T(8,128)(2,1)S(1)}, u32[]{:S(2)}, u32[]{:S(2)}) collective-permute-start(bf16[96,2432]{1,0:T(8,128)(2,1)S(1)} %get-tuple-element.133), channel_id=1, source_target_pairs={{0,3},{1,2},{2,1},{3,0},{4,7},{5,6},{6,5},{7,4},{8,11},{9,10},{10,... | collective-permute-start | bytes 1400840 | tf_op jit(solution)/shard_map/ppermute | solution.py:21
  7.3 11.5 %collective-permute-start.30 = (bf16[96,2304]{1,0:T(8,128)(2,1)S(1)}, bf16[96,2304]{1,0:T(8,128)(2,1)S(1)}, u32[]{:S(2)}, u32[]{:S(2)}) collective-permute-start(bf16[96,2304]{1,0:T(8,128)(2,1)S(1)} %get-tuple-element.121), channel_id=1, source_target_pairs={{0,4},{1,5},{2,6},{3,7},{4,0},{5,1},{6,2},{7,3},{8,12},{9,13},{10,... | collective-permute-start | bytes 1327112 | tf_op jit(solution)/shard_map/ppermute | solution.py:21
  19.0 6.3 %collective-permute-start.31 = (bf16[48,2304]{1,0:T(8,128)(2,1)S(1)}, bf16[48,2304]{1,0:T(8,128)(2,1)S(1)}, u32[]{:S(2)}, u32[]{:S(2)}) collective-permute-start(bf16[48,2304]{1,0:T(8,128)(2,1)S(1)} %get-tuple-element.123), channel_id=1, source_target_pairs={{0,1},{1,0},{2,3},{3,2},{4,5},{5,4},{6,7},{7,6},{8,9},{9,8},{10,11... | collective-permute-start | bytes 663560 | tf_op jit(solution)/shard_map/ppermute | solution.py:21
  20.6 7.3 %collective-permute-start.34 = (bf16[48,2432]{1,0:T(8,128)(2,1)S(1)}, bf16[48,2432]{1,0:T(8,128)(2,1)S(1)}, u32[]{:S(2)}, u32[]{:S(2)}) collective-permute-start(bf16[48,2432]{1,0:T(8,128)(2,1)S(1)} %get-tuple-element.129), channel_id=1, source_target_pairs={{0,3},{1,2},{2,1},{3,0},{4,7},{5,6},{6,5},{7,4},{8,11},{9,10},{10,... | collective-permute-start | bytes 700424 | tf_op jit(solution)/shard_map/ppermute | solution.py:21
  21.3 8.5 %collective-permute-start.37 = (bf16[48,2432]{1,0:T(8,128)(2,1)S(1)}, bf16[48,2432]{1,0:T(8,128)(2,1)S(1)}, u32[]{:S(2)}, u32[]{:S(2)}) collective-permute-start(bf16[48,2432]{1,0:T(8,128)(2,1)S(1)} %get-tuple-element.135), channel_id=1, source_target_pairs={{0,4},{1,5},{2,6},{3,7},{4,0},{5,1},{6,2},{7,3},{8,12},{9,13},{10,... | collective-permute-start | bytes 700424 | tf_op jit(solution)/shard_map/ppermute | solution.py:21
  25.3 6.2 %collective-permute-start.32 = (bf16[24,2304]{1,0:T(8,128)(2,1)S(1)}, bf16[24,2304]{1,0:T(8,128)(2,1)S(1)}, u32[]{:S(2)}, u32[]{:S(2)}) collective-permute-start(bf16[24,2304]{1,0:T(8,128)(2,1)S(1)} %get-tuple-element.125), channel_id=1, source_target_pairs={{0,3},{1,2},{2,1},{3,0},{4,7},{5,6},{6,5},{7,4},{8,11},{9,10},{10,... | collective-permute-start | bytes 331784 | tf_op jit(solution)/shard_map/ppermute | solution.py:21
  28.0 4.9 %collective-permute-start.35 = (bf16[24,2432]{1,0:T(8,128)(2,1)S(1)}, bf16[24,2432]{1,0:T(8,128)(2,1)S(1)}, u32[]{:S(2)}, u32[]{:S(2)}) collective-permute-start(bf16[24,2432]{1,0:T(8,128)(2,1)S(1)} %get-tuple-element.131), channel_id=1, source_target_pairs={{0,4},{1,5},{2,6},{3,7},{4,0},{5,1},{6,2},{7,3},{8,12},{9,13},{10,... | collective-permute-start | bytes 350216 | tf_op jit(solution)/shard_map/ppermute | solution.py:21
  29.9 4.9 %collective-permute-start.38 = (bf16[24,2432]{1,0:T(8,128)(2,1)S(1)}, bf16[24,2432]{1,0:T(8,128)(2,1)S(1)}, u32[]{:S(2)}, u32[]{:S(2)}) collective-permute-start(bf16[24,2432]{1,0:T(8,128)(2,1)S(1)} %get-tuple-element.137), channel_id=1, source_target_pairs={{0,1},{1,0},{2,3},{3,2},{4,5},{5,4},{6,7},{7,6},{8,9},{9,8},{10,11... | collective-permute-start | bytes 350216 | tf_op jit(solution)/shard_map/ppermute | solution.py:21
  34.8 31.4 %copy-start.4 = (f32[1,24,7168]{2,1,0:T(8,128)S(1)}, f32[1,24,7168]{2,1,0:T(8,128)}, u32[]{:S(2)}) copy-start(f32[1,24,7168]{2,1,0:T(8,128)} %param.18) | copy-start | bytes 2064388
  34.8 31.4 %copy-start.6 = (f32[1,24,7168]{2,1,0:T(8,128)S(1)}, f32[1,24,7168]{2,1,0:T(8,128)}, u32[]{:S(2)}) copy-start(f32[1,24,7168]{2,1,0:T(8,128)} %param.17) | copy-start | bytes 2064388
  36.2 16.4 %collective-permute-start.2 = (bf16[24,7168]{1,0:T(8,128)(2,1)S(1)}, bf16[24,7168]{1,0:T(8,128)(2,1)}, u32[]{:S(2)}, u32[]{:S(2)}) collective-permute-start(bf16[24,7168]{1,0:T(8,128)(2,1)S(1)} %param.2), channel_id=1, source_target_pairs={{0,32},{8,40},{16,48},{24,56},{32,0},{40,8},{48,16},{56,24},{64,96... | collective-permute-start | bytes 1032200 | tf_op jit(solution)/shard_map/cond/branch_2_fun/ppermute | solution.py:21
  53.7 9.7 %collective-permute-start.41 = (bf16[24,2432]{1,0:T(8,128)(2,1)S(1)}, bf16[24,2432]{1,0:T(8,128)(2,1)S(1)}, u32[]{:S(2)}, u32[]{:S(2)}) collective-permute-start(bf16[24,2432]{1,0:T(8,128)(2,1)S(1)} %get-tuple-element.161.here_ref), channel_id=1, source_target_pairs={{0,1},{1,0},{2,3},{3,2},{4,5},{5,4},{6,7},{7,6},{8,9},{9,8},{10,11... | collective-permute-start | bytes 350216 | tf_op jit(solution)/shard_map/ppermute | solution.py:21
  55.0 8.4 %collective-permute-start.40 = (bf16[24,2432]{1,0:T(8,128)(2,1)S(1)}, bf16[24,2432]{1,0:T(8,128)(2,1)S(1)}, u32[]{:S(2)}, u32[]{:S(2)}) collective-permute-start(bf16[24,2432]{1,0:T(8,128)(2,1)S(1)} %get-tuple-element.162.here_ref), channel_id=1, source_target_pairs={{0,4},{1,5},{2,6},{3,7},{4,0},{5,1},{6,2},{7,3},{8,12},{9,13},{10,... | collective-permute-start | bytes 350216 | tf_op jit(solution)/shard_map/ppermute | solution.py:21
  57.5 5.8 %collective-permute-start.39 = (bf16[24,2304]{1,0:T(8,128)(2,1)S(1)}, bf16[24,2304]{1,0:T(8,128)(2,1)S(1)}, u32[]{:S(2)}, u32[]{:S(2)}) collective-permute-start(bf16[24,2304]{1,0:T(8,128)(2,1)S(1)} %slice.12.here_ref), channel_id=1, source_target_pairs={{0,3},{1,2},{2,1},{3,0},{4,7},{5,6},{6,5},{7,4},{8,11},{9,10},{10,... | collective-permute-start | bytes 331784 | tf_op jit(solution)/shard_map/ppermute | solution.py:21
  63.4 7.9 %collective-permute-start.42 = (bf16[48,2304]{1,0:T(8,128)(2,1)S(1)}, bf16[48,2304]{1,0:T(8,128)(2,1)S(1)}, u32[]{:S(2)}, u32[]{:S(2)}) collective-permute-start(bf16[48,2304]{1,0:T(8,128)(2,1)S(1)} %join.6.here_ref), channel_id=1, source_target_pairs={{0,1},{1,0},{2,3},{3,2},{4,5},{5,4},{6,7},{7,6},{8,9},{9,8},{10,11... | collective-permute-start | bytes 663560 | tf_op jit(solution)/shard_map/ppermute | solution.py:21
  65.0 8.1 %collective-permute-start.43 = (bf16[48,2432]{1,0:T(8,128)(2,1)S(1)}, bf16[48,2432]{1,0:T(8,128)(2,1)S(1)}, u32[]{:S(2)}, u32[]{:S(2)}) collective-permute-start(bf16[48,2432]{1,0:T(8,128)(2,1)S(1)} %join.7.here_ref), channel_id=1, source_target_pairs={{0,3},{1,2},{2,1},{3,0},{4,7},{5,6},{6,5},{7,4},{8,11},{9,10},{10,... | collective-permute-start | bytes 700424 | tf_op jit(solution)/shard_map/ppermute | solution.py:21
  65.4 8.3 %collective-permute-start.44 = (bf16[48,2432]{1,0:T(8,128)(2,1)S(1)}, bf16[48,2432]{1,0:T(8,128)(2,1)S(1)}, u32[]{:S(2)}, u32[]{:S(2)}) collective-permute-start(bf16[48,2432]{1,0:T(8,128)(2,1)S(1)} %join.8.here_ref), channel_id=1, source_target_pairs={{0,4},{1,5},{2,6},{3,7},{4,0},{5,1},{6,2},{7,3},{8,12},{9,13},{10,... | collective-permute-start | bytes 700424 | tf_op jit(solution)/shard_map/ppermute | solution.py:21
  73.8 41.5 %collective-permute-start.16 = (bf16[96,2432]{1,0:T(8,128)(2,1)S(1)}, bf16[96,2432]{1,0:T(8,128)(2,1)}, u32[]{:S(2)}, u32[]{:S(2)}) collective-permute-start(bf16[96,2432]{1,0:T(8,128)(2,1)S(1)} %get-tuple-element.72), channel_id=1, source_target_pairs={{0,1},{1,0},{2,3},{3,2},{4,5},{5,4},{6,7},{7,6},{8,9},{9,8},{10,11... | collective-permute-start | bytes 1400840 | tf_op jit(solution)/shard_map/cond/branch_2_fun/ppermute | solution.py:21
  75.2 40.0 %collective-permute-start.17 = (bf16[96,2432]{1,0:T(8,128)(2,1)S(1)}, bf16[96,2432]{1,0:T(8,128)(2,1)}, u32[]{:S(2)}, u32[]{:S(2)}) collective-permute-start(bf16[96,2432]{1,0:T(8,128)(2,1)S(1)} %get-tuple-element.73), channel_id=1, source_target_pairs={{0,3},{1,2},{2,1},{3,0},{4,7},{5,6},{6,5},{7,4},{8,11},{9,10},{10,... | collective-permute-start | bytes 1400840 | tf_op jit(solution)/shard_map/cond/branch_2_fun/ppermute | solution.py:21
  76.8 38.5 %collective-permute-start.15 = (bf16[96,2304]{1,0:T(8,128)(2,1)S(1)}, bf16[96,2304]{1,0:T(8,128)(2,1)}, u32[]{:S(2)}, u32[]{:S(2)}) collective-permute-start(bf16[96,2304]{1,0:T(8,128)(2,1)S(1)} %get-tuple-element.71), channel_id=1, source_target_pairs={{0,4},{1,5},{2,6},{3,7},{4,0},{5,1},{6,2},{7,3},{8,12},{9,13},{10,... | collective-permute-start | bytes 1327112 | tf_op jit(solution)/shard_map/cond/branch_2_fun/ppermute | solution.py:21
  76.8 26.9 %collective-permute-start.18 = (bf16[24,7168]{1,0:T(8,128)(2,1)S(1)}, bf16[24,7168]{1,0:T(8,128)(2,1)}, u32[]{:S(2)}, u32[]{:S(2)}) collective-permute-start(bf16[24,7168]{1,0:T(8,128)(2,1)S(1)} %get-tuple-element.74), channel_id=1, source_target_pairs={{0,32},{8,40},{16,48},{24,56},{32,0},{40,8},{48,16},{56,24},{64,96... | collective-permute-start | bytes 1032200 | tf_op jit(solution)/shard_map/cond/branch_2_fun/ppermute | solution.py:21
  83.3 31.9 %collective-permute-start.19 = (bf16[24,7168]{1,0:T(8,128)(2,1)S(1)}, bf16[24,7168]{1,0:T(8,128)(2,1)}, u32[]{:S(2)}, u32[]{:S(2)}) collective-permute-start(bf16[24,7168]{1,0:T(8,128)(2,1)S(1)} %get-tuple-element.75), channel_id=1, source_target_pairs={{0,32},{8,40},{16,48},{24,56},{32,0},{40,8},{48,16},{56,24},{64,96... | collective-permute-start | bytes 1032200 | tf_op jit(solution)/shard_map/cond/branch_2_fun/ppermute | solution.py:21
  (5 other events, 52.3 us)
